TPU v7x, 512 devices: a whole 4x4x16 slice. The times are simulated.
512 devices in a mesh: band: 128 (over y, x_hi, z), grid: 4 (over x_lo, core).
Axes of the slice: x: 4 (x_hi: 2, x_lo: 2; x = x_hi * 2 + x_lo), y: 4, z: 16, core: 2. Of those that a mesh axis runs over, the one named last changes fastest.
Arguments:
- bands: float32 [128, 96, 96, 96], P('band', 'grid'), may hold values from -8 to 8
Outputs:
- exchange_term: float32 [128, 96, 96, 96], P('band', 'grid')
All inputs are finite; a program needn't handle non-finite values.
Results may differ from a plain program's by a relative error of at most 0.0003.
Values sent between devices are 32-bit elements; how exact they have to be, the bound alone decides.
A program may use at most 64 MiB of HBM per device.

v0:
```python
import jax
import jax.numpy as jnp
import numpy as np
from jax import lax
from jax.sharding import PartitionSpec as P

CYCLE = 2


EXACT = lax.Precision.HIGHEST


def from_behind(shard, axis, by):
    length = lax.axis_size(axis)
    return lax.ppermute(shard, axis, [(i, (i + by) % length) for i in range(length)])


def hartley(length):
    indices = jnp.arange(length, dtype=jnp.int32)
    phases = indices[:, None] * indices[None, :] % length
    angles = phases.astype(jnp.float32) * (2.0 * np.pi / length)
    return jnp.cos(angles) + jnp.sin(angles)


def wavenumber_sq(indices, length):
    folded = jnp.minimum(indices, length - indices).astype(jnp.float32)
    return folded * (2.0 * np.pi / length) * (folded * (2.0 * np.pi / length))


def coulomb(wave_sq, extent):
    screen = 4.0 * np.pi / extent
    guarded = jnp.where(wave_sq > 0, wave_sq, 1.0)
    screened = 0.2 * 4.0 * np.pi / guarded * (1.0 - jnp.exp(-guarded / (4.0 * screen * screen)))
    return jnp.where(wave_sq > 0, screened, 0.0)


def solve(density):
    planes, height, breadth = (density.shape[1], density.shape[2], density.shape[3])
    parts_grid = lax.axis_size("grid")
    planes_all = planes * parts_grid
    share_y = height // parts_grid
    offset_y = lax.axis_index("grid") * share_y
    table_z = hartley(breadth)
    table_y = hartley(height)
    table_x = hartley(planes_all)
    wave_sq = (
        wavenumber_sq(jnp.arange(planes_all, dtype=jnp.int32), planes_all)[:, None, None]
        + wavenumber_sq(offset_y + jnp.arange(share_y, dtype=jnp.int32), height)[None, :, None]
        + wavenumber_sq(jnp.arange(breadth, dtype=jnp.int32), breadth)[None, None, :]
    )
    kernel = coulomb(wave_sq, planes_all)
    spectrum = jnp.einsum("pxyz,zw->pxyw", density, table_z, precision=EXACT)
    spectrum = jnp.einsum("pxyz,yw->pxwz", spectrum, table_y, precision=EXACT)
    screened = (
        jnp.einsum(
            "xa,pxyz->payz",
            table_x,
            lax.all_to_all(spectrum, "grid", split_axis=2, concat_axis=1, tiled=True),
            precision=EXACT,
        )
        * kernel[None]
    )
    restored = jnp.einsum("xa,pxyz->payz", table_x, screened, precision=EXACT)
    spectrum = lax.all_to_all(restored, "grid", split_axis=1, concat_axis=2, tiled=True)
    spectrum = jnp.einsum("pxyz,yw->pxwz", spectrum, table_y, precision=EXACT)
    spectrum = jnp.einsum("pxyz,zw->pxyw", spectrum, table_z, precision=EXACT)
    return spectrum * (1.0 / (planes_all * height * breadth))


def collect(terms, picker):
    return jnp.einsum("pxyz,pi->ixyz", terms, picker, precision=EXACT)


def cross_pairs(orbitals, visitors):
    number = orbitals.shape[0]
    guests = visitors.shape[0]
    density = (orbitals[:, None] * visitors[None, :]).reshape(
        (number * guests,) + orbitals.shape[1:]
    )
    potential = solve(density).reshape((number, guests) + orbitals.shape[1:])
    return (
        jnp.sum(potential * visitors[None], axis=1),
        jnp.sum(potential * orbitals[:, None], axis=0),
    )


def shards(bands):
    number = bands.shape[0]
    leading, trailing = np.triu_indices(number)
    columns_id = np.arange(number)[None, :]
    pick_first = jnp.asarray((leading[:, None] == columns_id).astype(np.float32))
    pick_second = jnp.asarray(
        ((trailing[:, None] == columns_id) & (leading != trailing)[:, None]).astype(np.float32)
    )
    potential = solve(bands[leading] * bands[trailing])
    summed = collect(potential * bands[trailing], pick_first) + collect(
        potential * bands[leading], pick_second
    )
    visitor = bands
    for offset in range(1, CYCLE + 1):
        visitor = from_behind(visitor, "band", 1)
        nearby, remote = cross_pairs(bands, visitor)
        summed = summed + nearby + from_behind(remote, "band", -offset)
    return -summed


def solution(mesh):
    return jax.shard_map(
        shards,
        mesh=mesh,
        in_specs=(P("band", "grid", None, None),),
        out_specs=P("band", "grid", None, None),
        check_vma=False,
    )
```

profile of v0, /device:TPU:56, one launch (start us, length us, event | category | flops | bytes accessed | tf_op | source)
XLA Modules:
  0.0 249.8 jit_solution(9539997243134940302)
XLA Ops:
  0.0 3.8 %collective-permute-start = (f32[1,24,96,96]{3,2,1,0:T(8,128)}, f32[1,24,96,96]{3,2,1,0:T(8,128)S(1)}, u32[]{:S(2)}, u32[]{:S(2)}) collective-permute-start(f32[1,24,96,96]{3,2,1,0:T(8,128)} %param.9), channel_id=1, source_target_pairs={{0,4},{4,8},{8,12},{12,16},{16,20},{20,24},{24,28},{28,32},{32,36}... | collective-permute-start | bytes 2654216 | tf_op jit(solution)/shard_map/ppermute | solution.py:15
  3.8 2.6 %fusion.23 = f32[24,96,96]{2,1,0:T(8,128)S(1)} fusion(f32[1,24,96,96]{3,2,1,0:T(8,128)} %param.9), kind=kOutput, calls=%fused_computation.43 | convolution fusion | flops 255117312 | bytes 1769472 | tf_op jit(solution)/shard_map/pxyz,zw->pxyw/dot_general | solution.py:52
  6.4 1.3 convolution_bitcast_fusion.11
  7.7 1.7 copy.59
  9.4 4.4 %all-to-all-start = ((f32[1,24,96,96]{3,1,0,2:T(8,128)}), f32[1,24,96,96]{3,1,0,2:T(8,128)}, u32[]{:S(2)}, u32[]{:S(2)}) async-start(f32[1,24,96,96]{3,1,0,2:T(8,128)} %copy.59), calls=%async_computation | async-start | bytes 2359296 | tf_op jit(solution)/shard_map/all_to_all | solution.py:58
  13.9 15.9 %collective-permute-done = f32[1,24,96,96]{3,2,1,0:T(8,128)S(1)} collective-permute-done((f32[1,24,96,96]{3,2,1,0:T(8,128)}, f32[1,24,96,96]{3,2,1,0:T(8,128)S(1)}, u32[]{:S(2)}, u32[]{:S(2)}) %collective-permute-start) | collective-permute-done | bytes 884768 | tf_op jit(solution)/shard_map/ppermute | solution.py:15
  29.8 3.8 %collective-permute-start.2 = (f32[1,24,96,96]{3,2,1,0:T(8,128)S(1)}, f32[1,24,96,96]{3,2,1,0:T(8,128)S(1)}, u32[]{:S(2)}, u32[]{:S(2)}) collective-permute-start(f32[1,24,96,96]{3,2,1,0:T(8,128)S(1)} %collective-permute-done), channel_id=1, source_target_pairs={{0,4},{4,8},{8,12},{12,16},{16,20},{20,24},{24,28},{28,32},{32,36}... | collective-permute-start | bytes 2654216 | tf_op jit(solution)/shard_map/ppermute | solution.py:15
  33.6 1.3 fusion.21
  34.9 1.3 convolution_bitcast_fusion.7
  36.3 1.7 copy.67
  38.0 4.3 %all-to-all-start.2 = ((f32[1,24,96,96]{3,1,0,2:T(8,128)}), f32[1,24,96,96]{3,1,0,2:T(8,128)}, u32[]{:S(2)}, u32[]{:S(2)}) async-start(f32[1,24,96,96]{3,1,0,2:T(8,128)} %copy.67), calls=%async_computation.2 | async-start | bytes 2359296 | tf_op jit(solution)/shard_map/all_to_all | solution.py:58
  42.3 0.5 fusion.59
  42.9 24.8 %collective-permute-done.2 = f32[1,24,96,96]{3,2,1,0:T(8,128)S(1)} collective-permute-done((f32[1,24,96,96]{3,2,1,0:T(8,128)S(1)}, f32[1,24,96,96]{3,2,1,0:T(8,128)S(1)}, u32[]{:S(2)}, u32[]{:S(2)}) %collective-permute-start.2) | collective-permute-done | bytes 884768 | tf_op jit(solution)/shard_map/ppermute | solution.py:15
  67.6 1.3 fusion.15
  68.9 1.3 convolution_bitcast_fusion.3
  70.3 1.7 copy.75
  72.0 3.7 %all-to-all-start.4 = ((f32[1,24,96,96]{3,1,0,2:T(8,128)}), f32[1,24,96,96]{3,1,0,2:T(8,128)S(1)}, u32[]{:S(2)}, u32[]{:S(2)}) async-start(f32[1,24,96,96]{3,1,0,2:T(8,128)} %copy.75), calls=%async_computation.4 | async-start | bytes 2359296 | tf_op jit(solution)/shard_map/all_to_all | solution.py:58
  75.8 1.5 copy.68
  77.4 2.6 %fusion.7 = f32[96,24,96]{0,2,1:T(8,128)S(1)} fusion(f32[96,24,96]{2,1,0:T(8,128)S(1)} %bitcast.192, f32[96]{0:T(128)S(1)} %fusion.56, f32[96,24]{0,1:T(8,128)S(1)} %broadcast_add_fusion), kind=kOutput, calls=%fused_computation.24 | convolution fusion | flops 257107968 | bytes 1779072 | tf_op jit(solution)/shard_map/xa,pxyz->payz/dot_general | solution.py:55
  80.0 1.3 convolution_bitcast_fusion.5
  81.3 1.4 copy.71
  82.7 8.7 %all-to-all-done.4 = f32[1,24,96,96]{3,1,0,2:T(8,128)S(1)} async-done(((f32[1,24,96,96]{3,1,0,2:T(8,128)}), f32[1,24,96,96]{3,1,0,2:T(8,128)S(1)}, u32[]{:S(2)}, u32[]{:S(2)}) %all-to-all-start.4) | async-done | bytes 884768 | tf_op jit(solution)/shard_map/all_to_all | solution.py:58
  91.3 3.5 %all-to-all-start.3 = ((f32[1,96,24,96]{3,2,0,1:T(8,128)}), f32[1,96,24,96]{3,2,0,1:T(8,128)S(1)}, u32[]{:S(2)}, u32[]{:S(2)}) async-start(f32[1,96,24,96]{3,2,0,1:T(8,128)} %copy.71), calls=%async_computation.3 | async-start | bytes 2359296 | tf_op jit(solution)/shard_map/all_to_all | solution.py:64
  94.9 1.5 copy.60
  96.4 1.1 copy.61
  97.5 0.2 copy.76
  97.8 2.6 %fusion.9 = f32[96,24,96]{0,2,1:T(8,128)S(1)} fusion(f32[96,24,96]{2,1,0:T(8,128)S(1)} %bitcast.193, f32[96]{0:T(128)S(1)} %fusion.56, f32[96,24]{0,1:T(8,128)S(1)} %broadcast_add_fusion), kind=kOutput, calls=%fused_computation.26 | convolution fusion | flops 257107968 | bytes 1779072 | tf_op jit(solution)/shard_map/xa,pxyz->payz/dot_general | solution.py:55
  100.4 1.3 convolution_bitcast_fusion.1
  101.7 1.4 copy.79
  103.1 7.6 %all-to-all-done.3 = f32[1,96,24,96]{3,2,0,1:T(8,128)S(1)} async-done(((f32[1,96,24,96]{3,2,0,1:T(8,128)}), f32[1,96,24,96]{3,2,0,1:T(8,128)S(1)}, u32[]{:S(2)}, u32[]{:S(2)}) %all-to-all-start.3) | async-done | bytes 884768 | tf_op jit(solution)/shard_map/all_to_all | solution.py:64
  110.7 4.5 %all-to-all-start.5 = ((f32[1,96,24,96]{3,2,0,1:T(8,128)}), f32[1,96,24,96]{3,2,0,1:T(8,128)}, u32[]{:S(2)}, u32[]{:S(2)}) async-start(f32[1,96,24,96]{3,2,0,1:T(8,128)} %copy.79), calls=%async_computation.5 | async-start | bytes 2359296 | tf_op jit(solution)/shard_map/all_to_all | solution.py:64
  115.2 2.6 %fusion.5 = f32[96,24,96]{0,2,1:T(8,128)S(1)} fusion(f32[96,24,96]{2,1,0:T(8,128)S(1)} %bitcast.191, f32[96]{0:T(128)S(1)} %fusion.56, f32[96,24]{0,1:T(8,128)S(1)} %broadcast_add_fusion), kind=kOutput, calls=%fused_computation.22 | convolution fusion | flops 257107968 | bytes 1779072 | tf_op jit(solution)/shard_map/xa,pxyz->payz/dot_general | solution.py:55
  117.8 1.3 convolution_bitcast_fusion.9
  119.1 1.4 copy.63
  120.6 1.3 convolution_bitcast_fusion.4
  122.0 8.9 %all-to-all-done.5 = f32[1,96,24,96]{3,2,0,1:T(8,128)} async-done(((f32[1,96,24,96]{3,2,0,1:T(8,128)}), f32[1,96,24,96]{3,2,0,1:T(8,128)}, u32[]{:S(2)}, u32[]{:S(2)}) %all-to-all-start.5) | async-done | bytes 884768 | tf_op jit(solution)/shard_map/all_to_all | solution.py:64
  130.9 4.3 %all-to-all-start.1 = ((f32[1,96,24,96]{3,2,0,1:T(8,128)}), f32[1,96,24,96]{3,2,0,1:T(8,128)}, u32[]{:S(2)}, u32[]{:S(2)}) async-start(f32[1,96,24,96]{3,2,0,1:T(8,128)} %copy.63), calls=%async_computation.1 | async-start | bytes 2359296 | tf_op jit(solution)/shard_map/all_to_all | solution.py:64
  135.1 1.4 copy.80
  136.6 1.3 convolution_bitcast_fusion
  137.9 1.3 fusion.2
  139.2 3.1 %bitcast_multiply_fusion = (f32[1,24,96,96]{3,2,1,0:T(8,128)}, f32[1,24,96,96]{3,2,1,0:T(8,128)}, f32[24,96,96]{2,1,0:T(8,128)}) fusion(f32[1,24,96,96]{3,2,1,0:T(8,128)S(1)} %copy-done, f32[1,24,96,96]{3,2,1,0:T(8,128)S(1)} %fusion.2, f32[24,96,96]{2,1,0:T(8,128)S(1)} %convolution_bitcast_fusion.4), kind=kOutput, calls=%fused_computation.34 | convolution fusion | flops 255559680 | bytes 5308416 | tf_op jit(solution)/shard_map/pxyz,zw->pxyw/dot_general | solution.py:66
  142.3 26.7 %collective-permute-start.1 = (f32[1,24,96,96]{3,2,1,0:T(8,128)}, f32[1,24,96,96]{3,2,1,0:T(8,128)S(1)}, u32[]{:S(2)}, u32[]{:S(2)}) collective-permute-start(f32[1,24,96,96]{3,2,1,0:T(8,128)} %get-tuple-element.5), channel_id=1, source_target_pairs={{0,508},{4,0},{8,4},{12,8},{16,12},{20,16},{24,20},{28,24},{32,28}... | collective-permute-start | bytes 2654216 | tf_op jit(solution)/shard_map/ppermute | solution.py:15
  169.0 2.2 collective-permute-start.3
  171.2 1.5 copy.64
  172.8 1.3 convolution_bitcast_fusion.8
  174.1 26.4 %collective-permute-done.1 = f32[1,24,96,96]{3,2,1,0:T(8,128)S(1)} collective-permute-done((f32[1,24,96,96]{3,2,1,0:T(8,128)}, f32[1,24,96,96]{3,2,1,0:T(8,128)S(1)}, u32[]{:S(2)}, u32[]{:S(2)}) %collective-permute-start.1) | collective-permute-done | bytes 884768 | tf_op jit(solution)/shard_map/ppermute | solution.py:15
  200.5 45.3 %collective-permute-done.3 = f32[1,24,96,96]{3,2,1,0:T(8,128)} collective-permute-done((f32[1,24,96,96]{3,2,1,0:T(8,128)}, f32[1,24,96,96]{3,2,1,0:T(8,128)}, u32[]{:S(2)}, u32[]{:S(2)}) %collective-permute-start.3) | collective-permute-done | bytes 884768 | tf_op jit(solution)/shard_map/ppermute | solution.py:15
  245.8 4.0 %fusion.19 = f32[1,24,96,96]{3,2,1,0:T(8,128)} fusion(f32[1,24,96,96]{3,2,1,0:T(8,128)} %collective-permute-done.3, f32[1,24,96,96]{3,2,1,0:T(8,128)S(1)} %collective-permute-done.1, f32[24,96,96]{2,1,0:T(8,128)S(1)} %copy-done.5, f32[1,24,96,96]{3,2,1,0:T(8,128)S(1)} %copy-done.2, f32[1,24,96,96]{3,2,1,0:T(8,128)S(1)} %fusion.2, ...), kind=kOutput, calls=%fused_computation.38 | convolution fusion | flops 256886784 | bytes 7962624 | tf_op jit(solution)/shard_map/pxyz,zw->pxyw/dot_general | solution.py:66
  (24 shorter events, 0.4 us)
Async XLA Ops:
  0.0 29.8 %collective-permute-start = (f32[1,24,96,96]{3,2,1,0:T(8,128)}, f32[1,24,96,96]{3,2,1,0:T(8,128)S(1)}, u32[]{:S(2)}, u32[]{:S(2)}) collective-permute-start(f32[1,24,96,96]{3,2,1,0:T(8,128)} %param.9), channel_id=1, source_target_pairs={{0,4},{4,8},{8,12},{12,16},{16,20},{20,24},{24,28},{28,32},{32,36}... | collective-permute-start | bytes 2654216 | tf_op jit(solution)/shard_map/ppermute | solution.py:15
  9.4 24.2 %copy-start = (f32[1,24,96,96]{3,2,1,0:T(8,128)S(1)}, f32[1,24,96,96]{3,2,1,0:T(8,128)}, u32[]{:S(2)}) copy-start(f32[1,24,96,96]{3,2,1,0:T(8,128)} %param.9) | copy-start | bytes 2654212
  9.4 28.6 %all-to-all-start = ((f32[1,24,96,96]{3,1,0,2:T(8,128)}), f32[1,24,96,96]{3,1,0,2:T(8,128)}, u32[]{:S(2)}, u32[]{:S(2)}) async-start(f32[1,24,96,96]{3,1,0,2:T(8,128)} %copy.59), calls=%async_computation | async-start | bytes 2359296 | tf_op jit(solution)/shard_map/all_to_all | solution.py:58
  29.8 5.1 %copy-start.1 = (f32[1,24,96,96]{3,2,1,0:T(8,128)}, f32[1,24,96,96]{3,2,1,0:T(8,128)S(1)}, u32[]{:S(2)}) copy-start(f32[1,24,96,96]{3,2,1,0:T(8,128)S(1)} %collective-permute-done) | copy-start | bytes 2654212
  29.8 37.8 %collective-permute-start.2 = (f32[1,24,96,96]{3,2,1,0:T(8,128)S(1)}, f32[1,24,96,96]{3,2,1,0:T(8,128)S(1)}, u32[]{:S(2)}, u32[]{:S(2)}) collective-permute-start(f32[1,24,96,96]{3,2,1,0:T(8,128)S(1)} %collective-permute-done), channel_id=1, source_target_pairs={{0,4},{4,8},{8,12},{12,16},{16,20},{20,24},{24,28},{28,32},{32,36}... | collective-permute-start | bytes 2654216 | tf_op jit(solution)/shard_map/ppermute | solution.py:15
  38.0 34.0 %all-to-all-start.2 = ((f32[1,24,96,96]{3,1,0,2:T(8,128)}), f32[1,24,96,96]{3,1,0,2:T(8,128)}, u32[]{:S(2)}, u32[]{:S(2)}) async-start(f32[1,24,96,96]{3,1,0,2:T(8,128)} %copy.67), calls=%async_computation.2 | async-start | bytes 2359296 | tf_op jit(solution)/shard_map/all_to_all | solution.py:58
  67.6 1.3 copy-start.3
  72.0 3.7 %copy-start.7 = (f32[24]{0:T(128)S(1)}, f32[24]{0:T(128)}, u32[]{:S(2)}) copy-start(f32[24]{0:T(128)} %fusion.59) | copy-start | bytes 292
  72.0 19.3 %all-to-all-start.4 = ((f32[1,24,96,96]{3,1,0,2:T(8,128)}), f32[1,24,96,96]{3,1,0,2:T(8,128)S(1)}, u32[]{:S(2)}, u32[]{:S(2)}) async-start(f32[1,24,96,96]{3,1,0,2:T(8,128)} %copy.75), calls=%async_computation.4 | async-start | bytes 2359296 | tf_op jit(solution)/shard_map/all_to_all | solution.py:58
  91.3 19.3 %all-to-all-start.3 = ((f32[1,96,24,96]{3,2,0,1:T(8,128)}), f32[1,96,24,96]{3,2,0,1:T(8,128)S(1)}, u32[]{:S(2)}, u32[]{:S(2)}) async-start(f32[1,96,24,96]{3,2,0,1:T(8,128)} %copy.71), calls=%async_computation.3 | async-start | bytes 2359296 | tf_op jit(solution)/shard_map/all_to_all | solution.py:64
  103.1 12.1 %copy-start.6 = (f32[1,4,24,24,96]{4,3,2,1,0:T(8,128)S(1)}, f32[1,4,24,24,96]{4,3,2,1,0:T(8,128)}, u32[]{:S(2)}) copy-start(f32[1,4,24,24,96]{4,3,2,1,0:T(8,128)} %copy.61) | copy-start | bytes 2654212
  110.7 20.2 %all-to-all-start.5 = ((f32[1,96,24,96]{3,2,0,1:T(8,128)}), f32[1,96,24,96]{3,2,0,1:T(8,128)}, u32[]{:S(2)}, u32[]{:S(2)}) async-start(f32[1,96,24,96]{3,2,0,1:T(8,128)} %copy.79), calls=%async_computation.5 | async-start | bytes 2359296 | tf_op jit(solution)/shard_map/all_to_all | solution.py:64
  130.9 40.3 %all-to-all-start.1 = ((f32[1,96,24,96]{3,2,0,1:T(8,128)}), f32[1,96,24,96]{3,2,0,1:T(8,128)}, u32[]{:S(2)}, u32[]{:S(2)}) async-start(f32[1,96,24,96]{3,2,0,1:T(8,128)} %copy.63), calls=%async_computation.1 | async-start | bytes 2359296 | tf_op jit(solution)/shard_map/all_to_all | solution.py:64
  142.3 58.2 %collective-permute-start.1 = (f32[1,24,96,96]{3,2,1,0:T(8,128)}, f32[1,24,96,96]{3,2,1,0:T(8,128)S(1)}, u32[]{:S(2)}, u32[]{:S(2)}) collective-permute-start(f32[1,24,96,96]{3,2,1,0:T(8,128)} %get-tuple-element.5), channel_id=1, source_target_pairs={{0,508},{4,0},{8,4},{12,8},{16,12},{20,16},{24,20},{28,24},{32,28}... | collective-permute-start | bytes 2654216 | tf_op jit(solution)/shard_map/ppermute | solution.py:15
  169.0 76.8 %collective-permute-start.3 = (f32[1,24,96,96]{3,2,1,0:T(8,128)}, f32[1,24,96,96]{3,2,1,0:T(8,128)}, u32[]{:S(2)}, u32[]{:S(2)}) collective-permute-start(f32[1,24,96,96]{3,2,1,0:T(8,128)} %get-tuple-element.6), channel_id=1, source_target_pairs={{0,504},{4,508},{8,0},{12,4},{16,8},{20,12},{24,16},{28,20},{32,24... | collective-permute-start | bytes 2654216 | tf_op jit(solution)/shard_map/ppermute | solution.py:15
  171.2 74.6 %copy-start.5 = (f32[24,96,96]{2,1,0:T(8,128)S(1)}, f32[24,96,96]{2,1,0:T(8,128)}, u32[]{:S(2)}) copy-start(f32[24,96,96]{2,1,0:T(8,128)} %get-tuple-element.7) | copy-start | bytes 2654212
  172.7 73.0 %copy-start.2 = (f32[1,24,96,96]{3,2,1,0:T(8,128)S(1)}, f32[1,24,96,96]{3,2,1,0:T(8,128)}, u32[]{:S(2)}) copy-start(f32[1,24,96,96]{3,2,1,0:T(8,128)} %copy-done.1) | copy-start | bytes 2654212
  172.7 73.0 %copy-start.4 = (f32[1,24,96,96]{3,2,1,0:T(8,128)S(1)}, f32[1,24,96,96]{3,2,1,0:T(8,128)}, u32[]{:S(2)}) copy-start(f32[1,24,96,96]{3,2,1,0:T(8,128)} %copy-done.3) | copy-start | bytes 2654212
where the time goes:
time: 251 us; the launch traced here: 250 us
  waiting for transfers between devices  137 us (55%)
  starting transfers between devices  61.2 us (24%)
  matrix products  33.2 us (13%)
  local copies, waits for them, and re-layouts  16.9 us (7%)
    ppermute x4, waiting for transfers between devices, from_behind(): lax.ppermute(shard, axis, [(i, (i + by) % length) for i in range(length)])  112 us
    ppermute x4, starting transfers between devices, from_behind(): lax.ppermute(shard, axis, [(i, (i + by) % length) for i in range(length)])  36.5 us
    all_to_all x3, waiting for transfers between devices, solve(): lax.all_to_all(restored, 'grid', split_axis=1, concat_axis=2, tiled=True)  16.5 us
    all_to_all x3, starting transfers between devices, solve(): lax.all_to_all(spectrum, 'grid', split_axis=2, concat_axis=1, tiled=True)  12.4 us
    all_to_all x3, starting transfers between devices, solve(): lax.all_to_all(restored, 'grid', split_axis=1, concat_axis=2, tiled=True)  12.3 us
    all_to_all x3, waiting for transfers between devices, solve(): lax.all_to_all(spectrum, 'grid', split_axis=2, concat_axis=1, tiled=True)  8.68 us
    dot_general x3, matrix products, solve(): spectrum = jnp.einsum('pxyz,zw->pxyw', spectrum, table_z, precision=EXACT)  8.42 us
    dot_general x6, matrix products, solve(): spectrum = jnp.einsum('pxyz,yw->pxwz', spectrum, table_y, precision=EXACT)  8.06 us
  transfers between devices with their start and end apart: 10, of which 7 were waited for; matrix products, arithmetic and copies ran while one was open for 19% of the time, Pallas kernels for 0%

commit v1 on v0

v1 whole, which is shorter than its diff:
```python
import jax
import jax.numpy as jnp
import ml_dtypes
import numpy as np
from jax import lax
from jax.experimental import pallas as pl
from jax.experimental.pallas import tpu as pltpu
from jax.sharding import PartitionSpec as P

N = 96
PARTS = 4
PLANES = N // PARTS
CHUNKS = 3
DEEP = PLANES // CHUNKS
ROWS = 72
SHARE = ROWS // PARTS
LANES = 128
SCREEN = 4.0 * np.pi / N
MESH = pl.DeviceIdType.MESH
F32 = jnp.float32
BF16 = jnp.bfloat16


def tables():
    k = np.arange(N)
    angle = 2.0 * np.pi * (np.outer(k, k) % N) / N
    cas = np.cos(angle) + np.sin(angle)
    high = cas.astype(ml_dtypes.bfloat16)
    low = (cas - high.astype(np.float64)).astype(ml_dtypes.bfloat16)
    lanes = np.zeros((2 * LANES, 2 * LANES), ml_dtypes.bfloat16)
    for piece in range(2):
        lanes[piece * LANES : piece * LANES + N, :N] = high
        lanes[piece * LANES : piece * LANES + N, LANES : LANES + N] = low
    rows = np.block([[high, high], [low, low]])
    wave = (np.minimum(k, N - k) * (2.0 * np.pi / N)) ** 2
    j = np.arange(ROWS)[:, None]
    lane = np.arange(LANES)[None, :]
    first = lane < N
    ky = np.where(first, j, ROWS + j % 24)
    kz = np.where(first, lane, 32 * (j // 24) + lane - N)
    wave_yz = (wave[ky] + wave[kz]).astype(np.float32)
    wave_x = np.broadcast_to(wave[:, None], (N, LANES)).astype(np.float32)
    return lanes, rows, wave_yz, wave_x


def lane_ids(rows):
    return lax.broadcasted_iota(jnp.int32, (rows, LANES), 1)


def pack(plane):
    extra = plane[ROWS:]
    tail = lane_ids(24) >= N
    return jnp.concatenate(
        [
            jnp.where(tail, pltpu.roll(extra, N - 32 * c, 1), plane[24 * c : 24 * c + 24])
            for c in range(3)
        ],
        axis=0,
    )


def unpack(dense):
    lane = lane_ids(24)
    pieces = [pltpu.roll(dense[24 * c : 24 * c + 24], 32 * c + 32, 1) for c in range(3)]
    extra = jnp.where(lane < 32, pieces[0], jnp.where(lane < 64, pieces[1], pieces[2]))
    return jnp.concatenate([dense, extra], axis=0)


def split(x):
    high = x.astype(BF16)
    return high, (x - high.astype(F32)).astype(BF16)


def along_lanes(x, table):
    high, low = split(x)
    both = jnp.dot(
        jnp.concatenate([high, low], axis=1), table, preferred_element_type=F32
    )
    return both[:, :LANES] + both[:, LANES:]


def along_rows(x, table):
    high, low = split(x)
    both = jnp.dot(
        table, jnp.concatenate([high, low], axis=0), preferred_element_type=F32
    )
    return both[:N] + both[N:]


def exchange(
    b_ref, lanes_ref, rows_ref, wave_yz_ref, wave_x_ref, out_ref,
    own, below, above, total, coulomb,
    own_dense, below_dense, above_dense,
    to_above, to_below, from_below, from_above,
    sent, solved, back,
    local_sem, fwd_send, fwd_recv, ret_send, ret_recv,
    band_send, band_recv, term_send, term_recv,
):
    bands = lax.axis_size("band")
    me = lax.axis_index("band")
    part = lax.axis_index("grid")
    up = lax.rem(me + 1, bands)
    down = lax.rem(me + bands - 1, bands)

    barrier = pltpu.get_barrier_semaphore()
    for neighbour in (up, down):
        pl.semaphore_signal(
            barrier, inc=1, device_id={"band": neighbour}, device_id_type=MESH
        )
    for d in range(1, PARTS):
        pl.semaphore_signal(
            barrier,
            inc=1,
            device_id={"grid": lax.rem(part + d, PARTS)},
            device_id_type=MESH,
        )
    pl.semaphore_wait(barrier, PARTS + 1)

    def neighbours(k, up_src, up_dst, down_src, down_dst, send, recv):
        return (
            pltpu.make_async_remote_copy(
                up_src.at[k], up_dst.at[k], send.at[0, k], recv.at[0, k],
                device_id={"band": up}, device_id_type=MESH,
            ),
            pltpu.make_async_remote_copy(
                down_src.at[k], down_dst.at[k], send.at[1, k], recv.at[1, k],
                device_id={"band": down}, device_id_type=MESH,
            ),
        )

    def bands_out(k):
        return neighbours(
            k, own_dense, below_dense, own_dense, above_dense, band_send, band_recv
        )

    def terms_out(k):
        return neighbours(
            k, to_above, from_below, to_below, from_above, term_send, term_recv
        )

    def forward(s, k):
        copies = [
            pltpu.make_async_copy(
                sent.at[s, k, pl.ds(pl.multiple_of(part * SHARE * DEEP, 8), SHARE * DEEP)],
                solved.at[s, part * CHUNKS + k],
                local_sem.at[0, s, k],
            )
        ]
        for d in (2, 3, 1):
            peer = lax.rem(part + d, PARTS)
            copies.append(
                pltpu.make_async_remote_copy(
                    sent.at[s, k, pl.ds(pl.multiple_of(peer * SHARE * DEEP, 8), SHARE * DEEP)],
                    solved.at[s, part * CHUNKS + k],
                    fwd_send.at[s, d, k],
                    fwd_recv.at[s, d, k],
                    device_id={"grid": peer},
                    device_id_type=MESH,
                )
            )
        return copies

    def returned(s, k):
        copies = [
            pltpu.make_async_copy(
                solved.at[s, part * CHUNKS + k],
                back.at[s, k, pl.ds(pl.multiple_of(part * SHARE * DEEP, 8), SHARE * DEEP)],
                local_sem.at[1, s, k],
            )
        ]
        for d in (2, 3, 1):
            peer = lax.rem(part + d, PARTS)
            copies.append(
                pltpu.make_async_remote_copy(
                    solved.at[s, peer * CHUNKS + k],
                    back.at[s, k, pl.ds(pl.multiple_of(part * SHARE * DEEP, 8), SHARE * DEEP)],
                    ret_send.at[s, d, k],
                    ret_recv.at[s, d, k],
                    device_id={"grid": peer},
                    device_id_type=MESH,
                )
            )
        return copies

    def start(copies):
        for copy in copies:
            copy.start()

    def arrive(copies):
        copies[0].wait()
        for copy in copies[1:]:
            copy.wait_recv()

    def pairs_of_planes(body):
        lax.fori_loop(0, DEEP // 2, lambda i, c: (body(2 * i), c)[1], 0)

    def transform(s, k, i, first, second):
        z = along_lanes(jnp.concatenate([first, second], axis=0), lanes_ref[...])
        y = along_rows(jnp.concatenate([z[:N], z[N:]], axis=1), rows_ref[...])
        sent[s, k, pl.ds(i, ROWS, stride=DEEP), :] = pack(y[:, :LANES])
        sent[s, k, pl.ds(i + 1, ROWS, stride=DEEP), :] = pack(y[:, LANES:])

    def restore(s, k, i):
        first = unpack(back[s, k, pl.ds(i, ROWS, stride=DEEP), :])
        second = unpack(back[s, k, pl.ds(i + 1, ROWS, stride=DEEP), :])
        y = along_rows(jnp.concatenate([first, second], axis=1), rows_ref[...])
        return along_lanes(
            jnp.concatenate([y[:, :LANES], y[:, LANES:]], axis=0), lanes_ref[...]
        )

    def two(ref, x):
        return jnp.concatenate([ref[x], ref[x + 1]], axis=0)

    def dense_row(i):
        return pl.ds(pl.multiple_of(i * ROWS, 8), ROWS)

    for k in range(CHUNKS):

        def load(i, k=k):
            for x in (i, i + 1):
                plane = jnp.concatenate(
                    [b_ref[0, k * DEEP + x], jnp.zeros((N, LANES - N), F32)], axis=1
                )
                own[k * DEEP + x] = plane
                own_dense[k, dense_row(x), :] = pack(plane)

        pairs_of_planes(load)
        start(bands_out(k))

    for k in range(CHUNKS):

        def squared(i, k=k):
            first, second = own[k * DEEP + i], own[k * DEEP + i + 1]
            transform(0, k, i, first * first, second * second)

        pairs_of_planes(squared)
        start(forward(0, k))

    def table(j, c):
        wave_sq = wave_x_ref[...] + wave_yz_ref[pl.ds(part * SHARE + j, 1), :]
        guarded = jnp.where(wave_sq > 0, wave_sq, 1.0)
        screened = (-0.2 * 4.0 * np.pi / N**3) / guarded
        screened = screened * (1.0 - jnp.exp(guarded * (-1.0 / (4.0 * SCREEN * SCREEN))))
        coulomb[pl.ds(pl.multiple_of(j * N, 8), N), :] = jnp.where(wave_sq > 0, screened, 0.0)
        return c

    lax.fori_loop(0, SHARE, table, 0)

    for k in range(CHUNKS):
        for copy in bands_out(k):
            copy.wait_recv()

        def visitors(i, k=k):
            x = k * DEEP + i
            for e in range(2):
                above[x + e] = unpack(above_dense[k, dense_row(i + e), :])
                below[x + e] = unpack(below_dense[k, dense_row(i + e), :])
            transform(1, k, i, own[x] * above[x], own[x + 1] * above[x + 1])

        def apart(i, k=k):
            x = k * DEEP + i
            transform(2, k, i, below[x] * above[x], below[x + 1] * above[x + 1])

        pairs_of_planes(visitors)
        start(forward(1, k))
        pairs_of_planes(apart)
        start(forward(2, k))

    def solve(s):
        for k in range(CHUNKS):
            arrive(forward(s, k))

        def columns(i, c):
            at = [pl.ds(pl.multiple_of((2 * i + e) * DEEP, 8), DEEP) for e in range(2)]
            x = jnp.concatenate(
                [
                    jnp.concatenate([solved[s, p, rows, :] for p in range(N // DEEP)], axis=0)
                    for rows in at
                ],
                axis=1,
            )
            weight = jnp.concatenate(
                [
                    coulomb[pl.ds(pl.multiple_of((2 * i + e) * N, 8), N), :]
                    for e in range(2)
                ],
                axis=1,
            )
            x = along_rows(x, rows_ref[...]) * weight
            x = along_rows(x, rows_ref[...])
            for e, rows in enumerate(at):
                for p in range(N // DEEP):
                    solved[s, p, rows, :] = x[
                        p * DEEP : p * DEEP + DEEP, e * LANES : e * LANES + LANES
                    ]
            return c

        lax.fori_loop(0, SHARE // 2, columns, 0)

    solve(0)
    solve(1)
    start(returned(1, 0))
    solve(2)
    start(returned(2, 0))
    for k in range(1, CHUNKS):
        start(returned(1, k))
        start(returned(2, k))
    for k in range(CHUNKS):
        start(returned(0, k))

    for k in range(CHUNKS):
        arrive(returned(1, k))
        arrive(returned(2, k))

        def terms(i, k=k):
            x = k * DEEP + i
            near = restore(1, k, i)
            far = restore(2, k, i)
            next_band = two(above, x)
            result = near * next_band
            total[x] = result[:N]
            total[x + 1] = result[N:]
            upward = near * two(own, x) + far * two(below, x)
            downward = far * next_band
            for e in range(2):
                to_above[k, dense_row(i + e), :] = pack(upward[e * N : e * N + N])
                to_below[k, dense_row(i + e), :] = pack(downward[e * N : e * N + N])

        pairs_of_planes(terms)
        start(terms_out(k))

    for k in range(CHUNKS):
        arrive(returned(0, k))

        def same(i, k=k):
            x = k * DEEP + i
            result = restore(0, k, i) * two(own, x)
            total[x] += result[:N]
            total[x + 1] += result[N:]

        pairs_of_planes(same)

    for k in range(CHUNKS):
        for copy in terms_out(k):
            copy.wait_recv()

        def gather(i, k=k):
            for x in (i, i + 1):
                whole = (
                    total[k * DEEP + x]
                    + unpack(from_below[k, dense_row(x), :])
                    + unpack(from_above[k, dense_row(x), :])
                )
                out_ref[0, k * DEEP + x] = whole[:, :N]

        pairs_of_planes(gather)

    for k in range(CHUNKS):
        for copy in bands_out(k) + terms_out(k):
            copy.wait_send()
        for s in range(3):
            for copy in forward(s, k)[1:] + returned(s, k)[1:]:
                copy.wait_send()


def shards(bands):
    lanes, rows, wave_yz, wave_x = tables()
    vmem = pl.BlockSpec(memory_space=pltpu.VMEM)
    padded = pltpu.VMEM((PLANES, N, LANES), F32)
    dense = pltpu.VMEM((CHUNKS, DEEP * ROWS, LANES), F32)
    spectra = pltpu.VMEM((3, CHUNKS, ROWS * DEEP, LANES), F32)
    dma = pltpu.SemaphoreType.DMA
    return pl.pallas_call(
        exchange,
        out_shape=jax.ShapeDtypeStruct(bands.shape, bands.dtype),
        in_specs=[vmem] * 5,
        out_specs=vmem,
        scratch_shapes=[
            padded, padded, padded, padded,
            pltpu.VMEM((SHARE * N, LANES), F32),
            dense, dense, dense,
            dense, dense, dense, dense,
            spectra,
            pltpu.VMEM((3, N // DEEP, SHARE * DEEP, LANES), F32),
            spectra,
            dma((2, 3, CHUNKS)),
            dma((3, PARTS, CHUNKS)), dma((3, PARTS, CHUNKS)),
            dma((3, PARTS, CHUNKS)), dma((3, PARTS, CHUNKS)),
            dma((2, CHUNKS)), dma((2, CHUNKS)),
            dma((2, CHUNKS)), dma((2, CHUNKS)),
        ],
        compiler_params=pltpu.CompilerParams(
            collective_id=0, has_side_effects=True, vmem_limit_bytes=56 << 20
        ),
    )(bands, lanes, rows, wave_yz, wave_x)


def solution(mesh):
    return jax.shard_map(
        shards,
        mesh=mesh,
        in_specs=(P("band", "grid", None, None),),
        out_specs=P("band", "grid", None, None),
        check_vma=False,
    )
```

time: 251 us -> 124 us (0.49)
  the two profiles are of different devices: /device:TPU:56 before, /device:TPU:3 now
where the time goes in v1:
time: 124 us
  Pallas kernels  122 us (98%)
  local copies, waits for them, and re-layouts  2.36 us (2%)
    pallas_call x1, Pallas kernels, shards(): pl.pallas_call(exchange, out_shape=jax.ShapeDtypeStruct(bands.shape, band...  122 us

profile of v1, /device:TPU:3, one launch (start us, length us, event | category | flops | bytes accessed | tf_op | source)
XLA Modules:
  0.0 124.2 jit_solution(17207444262459969588)
XLA Ops:
  0.0 121.9 %shard_map.55 = f32[1,24,96,96]{3,2,1,0:T(8,128)} custom-call(f32[1,24,96,96]{3,2,1,0:T(8,128)} %b_ref.1, bf16[256,256]{1,0:T(8,128)(2,1)} %constant.8.clone.lanes_ref, bf16[192,192]{1,0:T(8,128)(2,1)} %constant.9.clone.rows_ref, f32[72,128]{1,0:T(8,128)} %constant.10.clone.wave_yz_ref, f32[96,128]{1,0:T(8,128)} %constant.11.clone.wave_x_ref), custom_call_target="tpu_custom_call" | custom-call | tf_op jit(solution)/shard_map/pallas_call | solution.py:373
  121.9 2.4 %copy.7 = f32[1,24,96,96]{3,2,1,0:T(8,128)} copy(f32[1,24,96,96]{3,2,1,0:T(8,128)} %shard_map.55) | data formatting | bytes 1769472

commit v2 on v1

v2 whole, which is shorter than its diff:
```python
import jax
import jax.numpy as jnp
import ml_dtypes
import numpy as np
from jax import lax
from jax.experimental import pallas as pl
from jax.experimental.pallas import tpu as pltpu
from jax.sharding import PartitionSpec as P

N = 96
PARTS = 4
PLANES = N // PARTS
CHUNKS = 3
DEEP = PLANES // CHUNKS
ROWS = 72
SHARE = ROWS // PARTS
LANES = 128
PIECES = DEEP // 2
COLUMN = 16
SCREEN = 4.0 * np.pi / N
MESH = pl.DeviceIdType.MESH
F32 = jnp.float32
BF16 = jnp.bfloat16


def tables():
    k = np.arange(N)
    angle = 2.0 * np.pi * (np.outer(k, k) % N) / N
    cas = np.cos(angle) + np.sin(angle)
    high = cas.astype(ml_dtypes.bfloat16)
    low = (cas - high.astype(np.float64)).astype(ml_dtypes.bfloat16)
    lanes = np.zeros((2 * LANES, 2 * LANES), ml_dtypes.bfloat16)
    for piece in range(2):
        lanes[piece * LANES : piece * LANES + N, :N] = high
        lanes[piece * LANES : piece * LANES + N, LANES : LANES + N] = low
    rows = np.block([[high, high], [low, low]])
    wave = (np.minimum(k, N - k) * (2.0 * np.pi / N)) ** 2
    j = np.arange(ROWS)[:, None]
    lane = np.arange(LANES)[None, :]
    first = lane < N
    ky = np.where(first, j, ROWS + j % 24)
    kz = np.where(first, lane, 32 * (j // 24) + lane - N)
    wave_yz = (wave[ky] + wave[kz]).astype(np.float32)
    wave_x = np.broadcast_to(wave[:, None], (N, LANES)).astype(np.float32)
    return lanes, rows, wave_yz, wave_x


def lane_ids(rows):
    return lax.broadcasted_iota(jnp.int32, (rows, LANES), 1)


def pack(plane):
    extra = plane[ROWS:]
    tail = lane_ids(24) >= N
    return jnp.concatenate(
        [
            jnp.where(tail, pltpu.roll(extra, N - 32 * c, 1), plane[24 * c : 24 * c + 24])
            for c in range(3)
        ],
        axis=0,
    )


def unpack(dense):
    lane = lane_ids(24)
    pieces = [pltpu.roll(dense[24 * c : 24 * c + 24], 32 * c + 32, 1) for c in range(3)]
    extra = jnp.where(lane < 32, pieces[0], jnp.where(lane < 64, pieces[1], pieces[2]))
    return jnp.concatenate([dense, extra], axis=0)


def split(x):
    high = x.astype(BF16)
    return high, (x - high.astype(F32)).astype(BF16)


def along_lanes(x, table):
    high, low = split(x)
    both = jnp.dot(
        jnp.concatenate([high, low], axis=1), table, preferred_element_type=F32
    )
    return both[:, :LANES] + both[:, LANES:]


def along_rows(x, table):
    high, low = split(x)
    both = jnp.dot(
        table, jnp.concatenate([high, low], axis=0), preferred_element_type=F32
    )
    return both[:N] + both[N:]


def exchange(
    b_ref, lanes_ref, rows_ref, wave_yz_ref, wave_x_ref, out_ref,
    own, visitor, total, coulomb,
    own_dense, visiting, outgoing, incoming,
    sent, solved, ready, back,
    fwd_send, fwd_recv, ret_send, ret_recv,
    band_send, band_recv, term_send, term_recv, passing, pass_send, pass_recv, here, there,
):
    bands = lax.axis_size("band")
    me = lax.axis_index("band")
    part = lax.axis_index("grid")
    level = lax.rem(me, COLUMN)
    first, last = level == 0, level == COLUMN - 1
    end = jnp.logical_or(first, last)
    host = jnp.logical_or(level == 1, level == COLUMN - 2)
    guest = jnp.where(level == 1, 0, 1)
    depth = COLUMN - 1 - level
    climbs = jnp.logical_and(level >= 2, level <= PIECES)
    sinks = jnp.logical_and(depth >= 2, depth <= PIECES)
    relays = range(2, PIECES + 1)

    def other(step):
        return {"band": lax.rem(me + step + bands, bands)}

    toward = {
        0: {"band": lax.rem(me + bands - 1, bands)},
        1: {"band": lax.rem(me + 1, bands)},
    }

    barrier = pltpu.get_barrier_semaphore()

    def greet(device):
        pl.semaphore_signal(barrier, inc=1, device_id=device, device_id_type=MESH)

    greet(toward[0])
    for d in range(1, PARTS):
        greet({"grid": lax.rem(part + d, PARTS)})

    @pl.when(jnp.logical_not(last))
    def _():
        greet(toward[1])

    @pl.when(climbs)
    def _():
        greet(other(-level - 1))

    @pl.when(sinks)
    def _():
        greet(other(depth))

    @pl.when(first)
    def _():
        for i in relays:
            greet(other(i))
            greet(other(-1 - i))

    pl.semaphore_wait(
        barrier,
        PARTS
        + jnp.where(first, 0, 1)
        + jnp.where(last, 2 * len(relays), 0)
        + jnp.where(jnp.logical_or(climbs, sinks), 1, 0),
    )

    @pl.when(last)
    def _():
        pl.semaphore_signal(here, inc=1, device_id=toward[1], device_id_type=MESH)
        for i in relays:
            pl.semaphore_signal(here, inc=1, device_id=other(-i), device_id_type=MESH)

    @pl.when(sinks)
    def _():
        pl.semaphore_signal(there, inc=1, device_id=other(depth + 1), device_id_type=MESH)

    def neighbour(k, side, src, dst, send, recv):
        return pltpu.make_async_remote_copy(
            src, dst.at[1 - side, k], send.at[side, k], recv.at[1 - side, k],
            device_id=toward[side], device_id_type=MESH,
        )

    def band_out(k, side):
        return neighbour(k, side, own_dense.at[k], visiting, band_send, band_recv)

    def term_out(k, side):
        return neighbour(k, side, outgoing.at[side, k], incoming, term_send, term_recv)

    def piece(i):
        return pl.ds(pl.multiple_of(i * 2 * ROWS, 8), 2 * ROWS)

    def term_pieces(k, side):
        way = 1 if side else -1
        return [
            pltpu.make_async_remote_copy(
                outgoing.at[side, k, piece(0)], incoming.at[1 - side, k, piece(0)],
                term_send.at[side, k], term_recv.at[1 - side, k],
                device_id=toward[side], device_id_type=MESH,
            )
        ] + [
            pltpu.make_async_remote_copy(
                outgoing.at[side, k, piece(i - 1)], passing.at[k],
                term_send.at[side, k], pass_recv.at[k],
                device_id=other(way * (1 + i)), device_id_type=MESH,
            )
            for i in relays
        ]

    def send_term(k, side):
        edge = last if side else first

        @pl.when(edge)
        def _():
            start(term_pieces(k, side))

        @pl.when(jnp.logical_not(edge))
        def _():
            term_out(k, side).start()

    def pass_on(k, side):
        at = depth if side else level
        return pltpu.make_async_remote_copy(
            passing.at[k], incoming.at[side, k, piece(at - 1)],
            pass_send.at[k], term_recv.at[side, k],
            device_id=other(depth if side else -level), device_id_type=MESH,
        )

    def pass_in(k):
        return pltpu.make_async_remote_copy(
            passing.at[k], passing.at[k], pass_send.at[k], pass_recv.at[k],
            device_id=toward[1], device_id_type=MESH,
        )

    def share(i):
        return pl.ds(pl.multiple_of(i * SHARE * DEEP, 8), SHARE * DEEP)

    def forward(s, k):
        return [
            pltpu.make_async_remote_copy(
                sent.at[s, k, share(lax.rem(part + d, PARTS))],
                solved.at[s, part * CHUNKS + k],
                fwd_send.at[s, d, k],
                fwd_recv.at[s, d, k],
                device_id={"grid": lax.rem(part + d, PARTS)},
                device_id_type=MESH,
            )
            for d in (2, 3, 1)
        ]

    def returned(s, k):
        return [
            pltpu.make_async_remote_copy(
                ready.at[s, lax.rem(part + d, PARTS) * CHUNKS + k],
                back.at[s, k, share(part)],
                ret_send.at[s, d, k],
                ret_recv.at[s, d, k],
                device_id={"grid": lax.rem(part + d, PARTS)},
                device_id_type=MESH,
            )
            for d in (2, 3, 1)
        ]

    def start(copies):
        for copy in copies:
            copy.start()

    def arrive(copies):
        for copy in copies:
            copy.wait_recv()

    def send_forward(s, k):
        start(forward(s, k))
        solved[s, part * CHUNKS + k] = sent[s, k, share(part), :]

    def send_back(s, k):
        start(returned(s, k))
        back[s, k, share(part), :] = ready[s, part * CHUNKS + k]

    def pairs_of_planes(body):
        lax.fori_loop(0, PIECES, lambda i, c: (body(i), c)[1], 0, unroll=True)

    def transform(s, k, i, first, second):
        z = along_lanes(jnp.concatenate([first, second], axis=0), lanes_ref[...])
        y = along_rows(jnp.concatenate([z[:N], z[N:]], axis=1), rows_ref[...])
        sent[s, k, pl.ds(2 * i, ROWS, stride=DEEP), :] = pack(y[:, :LANES])
        sent[s, k, pl.ds(2 * i + 1, ROWS, stride=DEEP), :] = pack(y[:, LANES:])

    def restore(s, k, i):
        first = unpack(back[s, k, pl.ds(2 * i, ROWS, stride=DEEP), :])
        second = unpack(back[s, k, pl.ds(2 * i + 1, ROWS, stride=DEEP), :])
        y = along_rows(jnp.concatenate([first, second], axis=1), rows_ref[...])
        return along_lanes(
            jnp.concatenate([y[:, :LANES], y[:, LANES:]], axis=0), lanes_ref[...]
        )

    def two(ref, *at):
        *head, x = at
        return jnp.concatenate([ref[(*head, x)], ref[(*head, x + 1)]], axis=0)

    def row(i, e):
        return pl.ds(pl.multiple_of((2 * i + e) * ROWS, 8), ROWS)

    def bring(side, k):
        band_out(k, 1 - side).wait_recv()

        def body(i):
            for e in range(2):
                visitor[side, k * DEEP + 2 * i + e] = unpack(visiting[side, k, row(i, e), :])

        pairs_of_planes(body)

    for k in range(CHUNKS):

        def load(i, k=k):
            for e in range(2):
                x = k * DEEP + 2 * i + e
                plane = jnp.concatenate(
                    [b_ref[0, x], jnp.zeros((N, LANES - N), F32)], axis=1
                )
                own[x] = plane
                own_dense[k, row(i, e), :] = pack(plane)

        pairs_of_planes(load)
        band_out(k, 1).start()

        @pl.when(jnp.logical_not(first))
        def _(k=k):
            band_out(k, 0).start()

    @pl.when(jnp.logical_not(end))
    def _():
        for k in range(CHUNKS):

            def squared(i, k=k):
                x = k * DEEP + 2 * i
                transform(0, k, i, own[x] * own[x], own[x + 1] * own[x + 1])

            pairs_of_planes(squared)
            send_forward(0, k)

    def table(j, c):
        wave_sq = wave_x_ref[...] + wave_yz_ref[pl.ds(part * SHARE + j, 1), :]
        guarded = jnp.where(wave_sq > 0, wave_sq, 1.0)
        screened = (-0.2 * 4.0 * np.pi / N**3) / guarded
        screened = screened * (1.0 - jnp.exp(guarded * (-1.0 / (4.0 * SCREEN * SCREEN))))
        coulomb[pl.ds(pl.multiple_of(j * N, 8), N), :] = jnp.where(wave_sq > 0, screened, 0.0)
        return c

    lax.fori_loop(0, SHARE, table, 0)

    for k in range(CHUNKS):
        bring(1, k)

        def beside(i, k=k):
            x = k * DEEP + 2 * i
            transform(1, k, i, own[x] * visitor[1, x], own[x + 1] * visitor[1, x + 1])

        pairs_of_planes(beside)
        send_forward(1, k)
        if k == 0:

            @pl.when(first)
            def _():
                pl.semaphore_wait(here, 1)
                for late in range(CHUNKS):
                    band_out(late, 0).start()

    for k in range(CHUNKS):
        bring(0, k)

        def apart(i, k=k):
            x = k * DEEP + 2 * i
            transform(
                2, k, i, visitor[0, x] * visitor[1, x], visitor[0, x + 1] * visitor[1, x + 1]
            )

        pairs_of_planes(apart)
        send_forward(2, k)

    @pl.when(host)
    def _():
        for k in range(CHUNKS):

            def squared(i, k=k):
                x = k * DEEP + 2 * i
                one, other = visitor[guest, x], visitor[guest, x + 1]
                transform(3, k, i, one * one, other * other)

            pairs_of_planes(squared)
            send_forward(3, k)

    def solve(s):
        for k in range(CHUNKS):
            arrive(forward(s, k))

        def columns(i, c):
            at = [pl.ds(pl.multiple_of((2 * i + e) * DEEP, 8), DEEP) for e in range(2)]
            x = jnp.concatenate(
                [
                    jnp.concatenate([solved[s, p, rows, :] for p in range(N // DEEP)], axis=0)
                    for rows in at
                ],
                axis=1,
            )
            weight = jnp.concatenate(
                [
                    coulomb[pl.ds(pl.multiple_of((2 * i + e) * N, 8), N), :]
                    for e in range(2)
                ],
                axis=1,
            )
            x = along_rows(x, rows_ref[...]) * weight
            x = along_rows(x, rows_ref[...])
            for e, rows in enumerate(at):
                for p in range(N // DEEP):
                    ready[s, p, rows, :] = x[
                        p * DEEP : p * DEEP + DEEP, e * LANES : e * LANES + LANES
                    ]
            return c

        lax.fori_loop(0, SHARE // 2, columns, 0, unroll=3)

    @pl.when(jnp.logical_not(end))
    def _():
        solve(0)

    solve(1)
    send_back(1, 0)
    solve(2)
    send_back(2, 0)
    send_back(1, 1)

    @pl.when(host)
    def _():
        solve(3)
        send_back(3, 0)

    send_back(2, 1)
    send_back(1, 2)

    @pl.when(host)
    def _():
        send_back(3, 1)

    send_back(2, 2)

    @pl.when(host)
    def _():
        send_back(3, 2)

    @pl.when(jnp.logical_not(end))
    def _():
        for k in range(CHUNKS):
            send_back(0, k)

    for k in range(CHUNKS):
        arrive(returned(1, k))
        arrive(returned(2, k))

        def terms(i, k=k):
            x = k * DEEP + 2 * i
            near = restore(1, k, i)
            far = restore(2, k, i)
            next_band = two(visitor, 1, x)
            result = near * next_band
            total[x] = result[:N]
            total[x + 1] = result[N:]
            upward = near * two(own, x) + far * two(visitor, 0, x)
            downward = far * next_band
            for e in range(2):
                outgoing[1, k, row(i, e), :] = pack(upward[e * N : e * N + N])
                outgoing[0, k, row(i, e), :] = pack(downward[e * N : e * N + N])

        pairs_of_planes(terms)

        @pl.when(host)
        def _(k=k):
            arrive(returned(3, k))

            def theirs(i):
                result = restore(3, k, i) * two(visitor, guest, k * DEEP + 2 * i)
                for e in range(2):
                    outgoing[guest, k, row(i, e), :] += pack(result[e * N : e * N + N])

            pairs_of_planes(theirs)

        if k == 0:

            @pl.when(first)
            def _():
                pl.semaphore_wait(there, len(relays))

        send_term(k, 1)
        send_term(k, 0)

    @pl.when(jnp.logical_not(end))
    def _():
        for k in range(CHUNKS):
            arrive(returned(0, k))

            def same(i, k=k):
                x = k * DEEP + 2 * i
                result = restore(0, k, i) * two(own, x)
                total[x] += result[:N]
                total[x + 1] += result[N:]

            pairs_of_planes(same)

    @pl.when(climbs)
    def _():
        for k in range(CHUNKS):
            pass_in(k).wait_recv()
            pass_on(k, 0).start()

    @pl.when(sinks)
    def _():
        pl.semaphore_wait(here, 1)
        for k in range(CHUNKS):
            pass_in(k).wait_recv()
            pass_on(k, 1).start()

    for k in range(CHUNKS):
        term_out(k, 1).wait_recv()
        term_out(k, 0).wait_recv()

        def gather(i, k=k):
            for e in range(2):
                x = k * DEEP + 2 * i + e
                whole = (
                    total[x]
                    + unpack(incoming[0, k, row(i, e), :])
                    + unpack(incoming[1, k, row(i, e), :])
                )
                out_ref[0, x] = whole[:, :N]

        pairs_of_planes(gather)

    def gone(s):
        for k in range(CHUNKS):
            for copy in forward(s, k) + returned(s, k):
                copy.wait_send()

    for k in range(CHUNKS):
        for side in range(2):
            band_out(k, side).wait_send()
            term_out(k, side).wait_send()
    gone(1)
    gone(2)

    @pl.when(jnp.logical_not(end))
    def _():
        gone(0)

    @pl.when(host)
    def _():
        gone(3)

    @pl.when(jnp.logical_or(climbs, sinks))
    def _():
        for k in range(CHUNKS):
            pass_in(k).wait_send()


def shards(bands):
    lanes, rows, wave_yz, wave_x = tables()
    vmem = pl.BlockSpec(memory_space=pltpu.VMEM)
    padded = pltpu.VMEM((PLANES, N, LANES), F32)
    dense = pltpu.VMEM((CHUNKS, DEEP * ROWS, LANES), F32)
    both = pltpu.VMEM((2, CHUNKS, DEEP * ROWS, LANES), F32)
    spectra = pltpu.VMEM((4, CHUNKS, ROWS * DEEP, LANES), F32)
    columns = pltpu.VMEM((4, N // DEEP, SHARE * DEEP, LANES), F32)
    dma = pltpu.SemaphoreType.DMA
    exchanged = dma((4, PARTS, CHUNKS))
    sides = dma((2, CHUNKS))
    return pl.pallas_call(
        exchange,
        out_shape=jax.ShapeDtypeStruct(bands.shape, bands.dtype),
        in_specs=[vmem] * 5,
        out_specs=vmem,
        scratch_shapes=[
            padded, pltpu.VMEM((2, PLANES, N, LANES), F32), padded,
            pltpu.VMEM((SHARE * N, LANES), F32),
            dense, both, both, both,
            spectra, columns, columns, spectra,
            exchanged, exchanged, exchanged, exchanged,
            sides, sides, sides, sides,
            pltpu.VMEM((CHUNKS, 2 * ROWS, LANES), F32), dma((CHUNKS,)), dma((CHUNKS,)),
            pltpu.SemaphoreType.REGULAR, pltpu.SemaphoreType.REGULAR,
        ],
        compiler_params=pltpu.CompilerParams(
            collective_id=0, has_side_effects=True, vmem_limit_bytes=56 << 20
        ),
    )(bands, lanes, rows, wave_yz, wave_x)


def solution(mesh):
    return jax.shard_map(
        shards,
        mesh=mesh,
        in_specs=(P("band", "grid", None, None),),
        out_specs=P("band", "grid", None, None),
        check_vma=False,
    )
```

time: 124 us -> 109 us (0.88)
  the two profiles are of different devices: /device:TPU:3 before, /device:TPU:1 now
where the time goes in v2:
time: 109 us
  Pallas kernels  107 us (98%)
  local copies, waits for them, and re-layouts  2.36 us (2%)
    pallas_call x1, Pallas kernels, shards(): pl.pallas_call(exchange, out_shape=jax.ShapeDtypeStruct(bands.shape, band...  107 us
    unnamed x1, local copies, waits for them, and re-layouts  2.36 us

profile of v2, /device:TPU:1, one launch (start us, length us, event | category | flops | bytes accessed | tf_op | source)
XLA Modules:
  0.0 109.1 jit_solution(9499873923972710098)
XLA Ops:
  0.0 106.8 %shard_map.55 = f32[1,24,96,96]{3,2,1,0:T(8,128)} custom-call(f32[1,24,96,96]{3,2,1,0:T(8,128)} %b_ref.1, bf16[256,256]{1,0:T(8,128)(2,1)} %constant.8.clone.lanes_ref, bf16[192,192]{1,0:T(8,128)(2,1)} %constant.9.clone.rows_ref, f32[72,128]{1,0:T(8,128)} %constant.10.clone.wave_yz_ref, f32[96,128]{1,0:T(8,128)} %constant.11.clone.wave_x_ref), custom_call_target="tpu_custom_call" | custom-call | tf_op jit(solution)/shard_map/pallas_call | solution.py:564
  106.8 2.4 %copy.7 = f32[1,24,96,96]{3,2,1,0:T(8,128)} copy(f32[1,24,96,96]{3,2,1,0:T(8,128)} %shard_map.55) | data formatting | bytes 1769472

commit v3 on v2

--- a/solution.py
+++ b/solution.py
@@ -95,23 +95,20 @@
     own_dense, visiting, outgoing, incoming,
     sent, solved, ready, back,
     fwd_send, fwd_recv, ret_send, ret_recv,
-    band_send, band_recv, term_send, term_recv, passing, pass_send, pass_recv, here, there,
+    band_send, band_recv, term_send, term_recv, here,
 ):
     bands = lax.axis_size("band")
     me = lax.axis_index("band")
     part = lax.axis_index("grid")
     level = lax.rem(me, COLUMN)
     first, last = level == 0, level == COLUMN - 1
-    end = jnp.logical_or(first, last)
-    host = jnp.logical_or(level == 1, level == COLUMN - 2)
-    guest = jnp.where(level == 1, 0, 1)
-    depth = COLUMN - 1 - level
-    climbs = jnp.logical_and(level >= 2, level <= PIECES)
-    sinks = jnp.logical_and(depth >= 2, depth <= PIECES)
-    relays = range(2, PIECES + 1)
-
-    def other(step):
-        return {"band": lax.rem(me + step + bands, bands)}
+    mate = jnp.where(level < COLUMN // 2, 0, 1)
+    host = level == 1
+    middle = level == COLUMN // 2 - 1
+    third = jnp.logical_or(host, middle)
+
+    def unless(condition):
+        return pl.when(jnp.logical_not(condition))
 
     toward = {
         0: {"band": lax.rem(me + bands - 1, bands)},
@@ -131,37 +128,11 @@
     def _():
         greet(toward[1])
 
-    @pl.when(climbs)
-    def _():
-        greet(other(-level - 1))
-
-    @pl.when(sinks)
-    def _():
-        greet(other(depth))
-
-    @pl.when(first)
-    def _():
-        for i in relays:
-            greet(other(i))
-            greet(other(-1 - i))
-
-    pl.semaphore_wait(
-        barrier,
-        PARTS
-        + jnp.where(first, 0, 1)
-        + jnp.where(last, 2 * len(relays), 0)
-        + jnp.where(jnp.logical_or(climbs, sinks), 1, 0),
-    )
+    pl.semaphore_wait(barrier, jnp.where(first, PARTS, PARTS + 1))
 
     @pl.when(last)
     def _():
         pl.semaphore_signal(here, inc=1, device_id=toward[1], device_id_type=MESH)
-        for i in relays:
-            pl.semaphore_signal(here, inc=1, device_id=other(-i), device_id_type=MESH)
-
-    @pl.when(sinks)
-    def _():
-        pl.semaphore_signal(there, inc=1, device_id=other(depth + 1), device_id_type=MESH)
 
     def neighbour(k, side, src, dst, send, recv):
         return pltpu.make_async_remote_copy(
@@ -174,51 +145,6 @@
 
     def term_out(k, side):
         return neighbour(k, side, outgoing.at[side, k], incoming, term_send, term_recv)
-
-    def piece(i):
-        return pl.ds(pl.multiple_of(i * 2 * ROWS, 8), 2 * ROWS)
-
-    def term_pieces(k, side):
-        way = 1 if side else -1
-        return [
-            pltpu.make_async_remote_copy(
-                outgoing.at[side, k, piece(0)], incoming.at[1 - side, k, piece(0)],
-                term_send.at[side, k], term_recv.at[1 - side, k],
-                device_id=toward[side], device_id_type=MESH,
-            )
-        ] + [
-            pltpu.make_async_remote_copy(
-                outgoing.at[side, k, piece(i - 1)], passing.at[k],
-                term_send.at[side, k], pass_recv.at[k],
-                device_id=other(way * (1 + i)), device_id_type=MESH,
-            )
-            for i in relays
-        ]
-
-    def send_term(k, side):
-        edge = last if side else first
-
-        @pl.when(edge)
-        def _():
-            start(term_pieces(k, side))
-
-        @pl.when(jnp.logical_not(edge))
-        def _():
-            term_out(k, side).start()
-
-    def pass_on(k, side):
-        at = depth if side else level
-        return pltpu.make_async_remote_copy(
-            passing.at[k], incoming.at[side, k, piece(at - 1)],
-            pass_send.at[k], term_recv.at[side, k],
-            device_id=other(depth if side else -level), device_id_type=MESH,
-        )
-
-    def pass_in(k):
-        return pltpu.make_async_remote_copy(
-            passing.at[k], passing.at[k], pass_send.at[k], pass_recv.at[k],
-            device_id=toward[1], device_id_type=MESH,
-        )
 
     def share(i):
         return pl.ds(pl.multiple_of(i * SHARE * DEEP, 8), SHARE * DEEP)
@@ -290,13 +216,24 @@
         return pl.ds(pl.multiple_of((2 * i + e) * ROWS, 8), ROWS)
 
     def bring(side, k):
-        band_out(k, 1 - side).wait_recv()
+        pltpu.make_async_remote_copy(
+            own_dense.at[k], visiting.at[side, k], band_send.at[0, k], band_recv.at[side, k],
+            device_id=toward[1], device_id_type=MESH,
+        ).wait_recv()
 
         def body(i):
             for e in range(2):
                 visitor[side, k * DEEP + 2 * i + e] = unpack(visiting[side, k, row(i, e), :])
 
         pairs_of_planes(body)
+
+    def alone(k):
+        def squared(i):
+            x = k * DEEP + 2 * i
+            transform(0, k, i, own[x] * own[x], own[x + 1] * own[x + 1])
+
+        pairs_of_planes(squared)
+        send_forward(0, k)
 
     for k in range(CHUNKS):
 
@@ -316,16 +253,16 @@
         def _(k=k):
             band_out(k, 0).start()
 
-    @pl.when(jnp.logical_not(end))
-    def _():
-        for k in range(CHUNKS):
-
-            def squared(i, k=k):
-                x = k * DEEP + 2 * i
-                transform(0, k, i, own[x] * own[x], own[x + 1] * own[x + 1])
-
-            pairs_of_planes(squared)
-            send_forward(0, k)
+    @pl.when(first)
+    def _():
+        pl.semaphore_wait(here, 1)
+        for k in range(CHUNKS):
+            band_out(k, 0).start()
+
+    @unless(jnp.logical_or(first, last))
+    def _():
+        for k in range(CHUNKS):
+            alone(k)
 
     def table(j, c):
         wave_sq = wave_x_ref[...] + wave_yz_ref[pl.ds(part * SHARE + j, 1), :]
@@ -337,25 +274,27 @@
 
     lax.fori_loop(0, SHARE, table, 0)
 
+    @unless(last)
+    def _():
+        for k in range(CHUNKS):
+            bring(mate, k)
+
+            def beside(i, k=k):
+                x = k * DEEP + 2 * i
+                transform(
+                    1, k, i, own[x] * visitor[mate, x], own[x + 1] * visitor[mate, x + 1]
+                )
+
+            pairs_of_planes(beside)
+            send_forward(1, k)
+
     for k in range(CHUNKS):
-        bring(1, k)
-
-        def beside(i, k=k):
-            x = k * DEEP + 2 * i
-            transform(1, k, i, own[x] * visitor[1, x], own[x + 1] * visitor[1, x + 1])
-
-        pairs_of_planes(beside)
-        send_forward(1, k)
-        if k == 0:
-
-            @pl.when(first)
-            def _():
-                pl.semaphore_wait(here, 1)
-                for late in range(CHUNKS):
-                    band_out(late, 0).start()
-
-    for k in range(CHUNKS):
-        bring(0, k)
+
+        @pl.when(last)
+        def _(k=k):
+            bring(1, k)
+
+        bring(1 - mate, k)
 
         def apart(i, k=k):
             x = k * DEEP + 2 * i
@@ -370,13 +309,29 @@
     def _():
         for k in range(CHUNKS):
 
-            def squared(i, k=k):
-                x = k * DEEP + 2 * i
-                one, other = visitor[guest, x], visitor[guest, x + 1]
+            def guest(i, k=k):
+                x = k * DEEP + 2 * i
+                one, other = visitor[0, x], visitor[0, x + 1]
                 transform(3, k, i, one * one, other * other)
 
-            pairs_of_planes(squared)
+            pairs_of_planes(guest)
             send_forward(3, k)
+
+    @pl.when(middle)
+    def _():
+        for k in range(CHUNKS):
+
+            def bridge(i, k=k):
+                x = k * DEEP + 2 * i
+                transform(3, k, i, own[x] * visitor[1, x], own[x + 1] * visitor[1, x + 1])
+
+            pairs_of_planes(bridge)
+            send_forward(3, k)
+
+    @pl.when(last)
+    def _():
+        for k in range(CHUNKS):
+            alone(k)
 
     def solve(s):
         for k in range(CHUNKS):
@@ -409,80 +364,120 @@
 
         lax.fori_loop(0, SHARE // 2, columns, 0, unroll=3)
 
-    @pl.when(jnp.logical_not(end))
+    @unless(jnp.logical_or(first, last))
     def _():
         solve(0)
 
-    solve(1)
-    send_back(1, 0)
+    @unless(last)
+    def _():
+        solve(1)
+        send_back(1, 0)
+
     solve(2)
     send_back(2, 0)
-    send_back(1, 1)
-
-    @pl.when(host)
+
+    @unless(last)
+    def _():
+        send_back(1, 1)
+
+    @pl.when(third)
     def _():
         solve(3)
         send_back(3, 0)
 
     send_back(2, 1)
-    send_back(1, 2)
-
-    @pl.when(host)
+
+    @unless(last)
+    def _():
+        send_back(1, 2)
+
+    @pl.when(third)
     def _():
         send_back(3, 1)
 
     send_back(2, 2)
 
-    @pl.when(host)
+    @pl.when(third)
     def _():
         send_back(3, 2)
 
-    @pl.when(jnp.logical_not(end))
+    @pl.when(last)
+    def _():
+        solve(0)
+
+    @unless(first)
     def _():
         for k in range(CHUNKS):
             send_back(0, k)
 
+    upper = jnp.where(mate == 1, 1.0, 0.0).astype(F32)
+
+    def put(side, k, i, planes, add=False):
+        for e in range(2):
+            dense = pack(planes[e * N : e * N + N])
+            if add:
+                dense = dense + outgoing[side, k, row(i, e), :]
+            outgoing[side, k, row(i, e), :] = dense
+
     for k in range(CHUNKS):
-        arrive(returned(1, k))
         arrive(returned(2, k))
 
-        def terms(i, k=k):
-            x = k * DEEP + 2 * i
-            near = restore(1, k, i)
-            far = restore(2, k, i)
-            next_band = two(visitor, 1, x)
-            result = near * next_band
-            total[x] = result[:N]
-            total[x + 1] = result[N:]
-            upward = near * two(own, x) + far * two(visitor, 0, x)
-            downward = far * next_band
-            for e in range(2):
-                outgoing[1, k, row(i, e), :] = pack(upward[e * N : e * N + N])
-                outgoing[0, k, row(i, e), :] = pack(downward[e * N : e * N + N])
-
-        pairs_of_planes(terms)
+        @unless(last)
+        def _(k=k):
+            arrive(returned(1, k))
+
+            def terms(i):
+                x = k * DEEP + 2 * i
+                near = restore(1, k, i)
+                far = restore(2, k, i)
+                result = near * two(visitor, mate, x)
+                total[x] = result[:N]
+                total[x + 1] = result[N:]
+                near = near * two(own, x)
+                put(1, k, i, far * two(visitor, 0, x) + near * upper)
+                put(0, k, i, far * two(visitor, 1, x) + near * (1.0 - upper))
+
+            pairs_of_planes(terms)
+
+        @pl.when(last)
+        def _(k=k):
+            def terms(i):
+                x = k * DEEP + 2 * i
+                far = restore(2, k, i)
+                total[x] = jnp.zeros((N, LANES), F32)
+                total[x + 1] = jnp.zeros((N, LANES), F32)
+                put(1, k, i, far * two(visitor, 0, x))
+                put(0, k, i, far * two(visitor, 1, x))
+
+            pairs_of_planes(terms)
 
         @pl.when(host)
         def _(k=k):
             arrive(returned(3, k))
 
             def theirs(i):
-                result = restore(3, k, i) * two(visitor, guest, k * DEEP + 2 * i)
-                for e in range(2):
-                    outgoing[guest, k, row(i, e), :] += pack(result[e * N : e * N + N])
+                put(0, k, i, restore(3, k, i) * two(visitor, 0, k * DEEP + 2 * i), add=True)
 
             pairs_of_planes(theirs)
 
-        if k == 0:
-
-            @pl.when(first)
-            def _():
-                pl.semaphore_wait(there, len(relays))
-
-        send_term(k, 1)
-        send_term(k, 0)
-
-    @pl.when(jnp.logical_not(end))
+        @pl.when(middle)
+        def _(k=k):
+            arrive(returned(3, k))
+
+            def across(i):
+                x = k * DEEP + 2 * i
+                near = restore(3, k, i)
+                result = near * two(visitor, 1, x)
+                total[x] += result[:N]
+                total[x + 1] += result[N:]
+                put(1, k, i, near * two(own, x), add=True)
+
+            pairs_of_planes(across)
+
+        term_out(k, 1).start()
+        term_out(k, 0).start()
+
+    @unless(first)
     def _():
         for k in range(CHUNKS):
             arrive(returned(0, k))
@@ -494,19 +489,6 @@
                 total[x + 1] += result[N:]
 
             pairs_of_planes(same)
-
-    @pl.when(climbs)
-    def _():
-        for k in range(CHUNKS):
-            pass_in(k).wait_recv()
-            pass_on(k, 0).start()
-
-    @pl.when(sinks)
-    def _():
-        pl.semaphore_wait(here, 1)
-        for k in range(CHUNKS):
-            pass_in(k).wait_recv()
-            pass_on(k, 1).start()
 
     for k in range(CHUNKS):
         term_out(k, 1).wait_recv()
@@ -533,21 +515,19 @@
         for side in range(2):
             band_out(k, side).wait_send()
             term_out(k, side).wait_send()
-    gone(1)
     gone(2)
 
-    @pl.when(jnp.logical_not(end))
+    @unless(last)
+    def _():
+        gone(1)
+
+    @unless(first)
     def _():
         gone(0)
 
-    @pl.when(host)
+    @pl.when(third)
     def _():
         gone(3)
-
-    @pl.when(jnp.logical_or(climbs, sinks))
-    def _():
-        for k in range(CHUNKS):
-            pass_in(k).wait_send()
 
 
 def shards(bands):
@@ -573,8 +553,7 @@
             spectra, columns, columns, spectra,
             exchanged, exchanged, exchanged, exchanged,
             sides, sides, sides, sides,
-            pltpu.VMEM((CHUNKS, 2 * ROWS, LANES), F32), dma((CHUNKS,)), dma((CHUNKS,)),
-            pltpu.SemaphoreType.REGULAR, pltpu.SemaphoreType.REGULAR,
+            pltpu.SemaphoreType.REGULAR,
         ],
         compiler_params=pltpu.CompilerParams(
             collective_id=0, has_side_effects=True, vmem_limit_bytes=56 << 20

time: 109 us -> 105 us (0.963)
  the two profiles are of different devices: /device:TPU:1 before, /device:TPU:41 now
where the time goes in v3:
time: 105 us
  Pallas kernels  102 us (97%)
  local copies, waits for them, and re-layouts  2.36 us (2%)
    pallas_call x1, Pallas kernels, shards(): pl.pallas_call(exchange, out_shape=jax.ShapeDtypeStruct(bands.shape, band...  102 us
    unnamed x1, local copies, waits for them, and re-layouts  2.36 us

profile of v3, /device:TPU:41, one launch (start us, length us, event | category | flops | bytes accessed | tf_op | source)
XLA Modules:
  0.0 104.8 jit_solution(15182970250322903835)
XLA Ops:
  0.0 102.5 %shard_map.55 = f32[1,24,96,96]{3,2,1,0:T(8,128)} custom-call(f32[1,24,96,96]{3,2,1,0:T(8,128)} %b_ref.1, bf16[256,256]{1,0:T(8,128)(2,1)} %constant.8.clone.lanes_ref, bf16[192,192]{1,0:T(8,128)(2,1)} %constant.9.clone.rows_ref, f32[72,128]{1,0:T(8,128)} %constant.10.clone.wave_yz_ref, f32[96,128]{1,0:T(8,128)} %constant.11.clone.wave_x_ref), custom_call_target="tpu_custom_call" | custom-call | tf_op jit(solution)/shard_map/pallas_call | solution.py:544
  102.5 2.4 %copy.7 = f32[1,24,96,96]{3,2,1,0:T(8,128)} copy(f32[1,24,96,96]{3,2,1,0:T(8,128)} %shard_map.55) | data formatting | bytes 1769472

commit v4 on v3

--- a/solution.py
+++ b/solution.py
@@ -327,11 +327,6 @@
 
             pairs_of_planes(bridge)
             send_forward(3, k)
-
-    @pl.when(last)
-    def _():
-        for k in range(CHUNKS):
-            alone(k)
 
     def solve(s):
         for k in range(CHUNKS):
@@ -403,6 +398,8 @@
 
     @pl.when(last)
     def _():
+        for k in range(CHUNKS):
+            alone(k)
         solve(0)
 
     @unless(first)

time: 105 us -> 120 us (1.14)
  the two profiles are of different devices: /device:TPU:41 before, /device:TPU:1 now
where the time goes in v4:
time: 120 us
  Pallas kernels  118 us (98%)
  local copies, waits for them, and re-layouts  2.36 us (2%)
    pallas_call x1, Pallas kernels, shards(): pl.pallas_call(exchange, out_shape=jax.ShapeDtypeStruct(bands.shape, band...  118 us

profile of v4, /device:TPU:1, one launch (start us, length us, event | category | flops | bytes accessed | tf_op | source)
XLA Modules:
  0.0 120.1 jit_solution(7944397872476351524)
XLA Ops:
  0.0 117.7 %shard_map.55 = f32[1,24,96,96]{3,2,1,0:T(8,128)} custom-call(f32[1,24,96,96]{3,2,1,0:T(8,128)} %b_ref.1, bf16[256,256]{1,0:T(8,128)(2,1)} %constant.8.clone.lanes_ref, bf16[192,192]{1,0:T(8,128)(2,1)} %constant.9.clone.rows_ref, f32[72,128]{1,0:T(8,128)} %constant.10.clone.wave_yz_ref, f32[96,128]{1,0:T(8,128)} %constant.11.clone.wave_x_ref), custom_call_target="tpu_custom_call" | custom-call | tf_op jit(solution)/shard_map/pallas_call | solution.py:541
  117.7 2.4 %copy.7 = f32[1,24,96,96]{3,2,1,0:T(8,128)} copy(f32[1,24,96,96]{3,2,1,0:T(8,128)} %shard_map.55) | data formatting | bytes 1769472
